TPU v7x, 32 devices: a whole 2x2x4 slice. The times are simulated.
32 devices in a mesh: head: 4 (over y, x), pb: 8 (over z, core).
Axes of the slice: x: 2, y: 2, z: 4, core: 2. Of those that a mesh axis runs over, the one named last changes fastest.
Arguments:
- pair: bfloat16 [512, 512, 128], P('pb', 'head'), may hold values from -6 to 6
- tokens: bfloat16 [512, 768], P('pb'), may hold values from -6 to 6
- token_mask: int32 [512], replicated, may hold values from 0 to 1, as said below
- w_gu: bfloat16 [2, 128, 512], replicated, may hold values from -0.5 to 0.5
- w_down: bfloat16 [2, 256, 128], replicated, may hold values from -0.375 to 0.375
- w_bias: bfloat16 [128, 32], replicated, may hold values from -0.5 to 0.5
- w_q: bfloat16 [2, 768, 768], P(None, None, 'head'), may hold values from -0.21875 to 0.21875
- w_k: bfloat16 [2, 768, 768], P(None, None, 'head'), may hold values from -0.21875 to 0.21875
- w_v: bfloat16 [2, 768, 768], P(None, None, 'head'), may hold values from -0.21875 to 0.21875
- w_gate: bfloat16 [2, 768, 768], P(None, None, 'head'), may hold values from -0.21875 to 0.21875
- w_out: bfloat16 [2, 768, 768], P(None, 'head'), may hold values from -0.875 to 0.875
Outputs:
- updated: bfloat16 [512, 768], P('pb')
Inputs may be any that keep to these rules, and one draw needn't show every extreme that they name: `token_mask`: ones on a prefix of the tokens and zeros after it; at least 128 ones and at least one zero.
All inputs are finite; a program needn't handle non-finite values.
Results may differ from a plain program's by a relative error of at most 0.019.
Values may be sent and summed in bfloat16 or wider, within the bound.
A program may use at most 64 MiB of HBM per device.

v0:
```python
import math

import jax
import jax.numpy as jnp
from jax import lax
from jax.sharding import PartitionSpec as P

TRANS = 2
LAYERS = 2
HD = 48


def normalize(values):
    values = values.astype(jnp.float32)
    center = values - jnp.mean(values, axis=-1, keepdims=True)
    spread = jnp.mean(center * center, axis=-1, keepdims=True)
    return center * lax.rsqrt(spread + 1e-05)


def transition(pair_rows, w_updown, w_back):
    hidden_units = w_back.shape[0]
    normed = normalize(pair_rows).astype(jnp.bfloat16)
    mixed = jnp.dot(normed, w_updown, preferred_element_type=jnp.float32)
    hidden = (jax.nn.silu(mixed[:, :hidden_units]) * mixed[:, hidden_units:]).astype(jnp.bfloat16)
    summed = pair_rows.astype(jnp.float32) + jnp.dot(
        hidden, w_back, preferred_element_type=jnp.float32
    )
    return summed.astype(jnp.bfloat16)


def on_device(pair, tokens, token_mask, w_gu, w_down, w_bias, w_q, w_k, w_v, w_gate, w_out):
    row_count, col_count, channels = pair.shape
    entries = row_count * col_count
    block_rows = math.gcd(entries, 2048)
    blocked = pair.reshape(entries // block_rows, block_rows, channels)
    heads_all = w_bias.shape[1] // LAYERS

    def project(pair_block):
        current = pair_block
        for section_index in range(TRANS):
            current = transition(current, w_gu[section_index], w_down[section_index])
        normed = normalize(current).astype(jnp.bfloat16)
        return jnp.einsum("rc,cj->jr", normed, w_bias, preferred_element_type=jnp.float32).astype(
            jnp.bfloat16
        )

    projected = lax.map(project, blocked)
    columns_first = jnp.transpose(projected, (1, 0, 2))
    bias_local = columns_first.reshape(LAYERS, heads_all, row_count, col_count)
    layer_bias = [
        lax.all_to_all(bias_local[layer_index], "head", split_axis=0, concat_axis=2, tiled=True)
        for layer_index in range(LAYERS)
    ]
    is_real = token_mask == 1
    query_real = lax.dynamic_slice_in_dim(
        token_mask, lax.axis_index("pb") * row_count, row_count, 0
    ).astype(jnp.float32)
    local_width = w_q.shape[2]
    local_heads = local_width // HD
    scale_factor = 1.0 / HD**0.5
    state = tokens.astype(jnp.float32)
    for layer_index in range(LAYERS):
        normed = normalize(state).astype(jnp.bfloat16)
        queries = jnp.dot(normed, w_q[layer_index], preferred_element_type=jnp.float32).astype(
            jnp.bfloat16
        )
        key_proj = jnp.dot(normed, w_k[layer_index], preferred_element_type=jnp.float32).astype(
            jnp.bfloat16
        )
        value_proj = jnp.dot(normed, w_v[layer_index], preferred_element_type=jnp.float32).astype(
            jnp.bfloat16
        )
        gate_vals = jnp.dot(normed, w_gate[layer_index], preferred_element_type=jnp.float32).astype(
            jnp.bfloat16
        )
        packed = jnp.concatenate([key_proj, value_proj], axis=1)
        query_heads = queries.astype(jnp.float32).reshape(row_count, local_heads, HD)
        bias_now = layer_bias[layer_index]
        every_key = lax.all_gather(packed, "pb", axis=0, tiled=True)
        piece_len = every_key.shape[0]
        key_heads = (
            every_key[:, :local_width].astype(jnp.float32).reshape(piece_len, local_heads, HD)
        )
        value_heads = (
            every_key[:, local_width:].astype(jnp.float32).reshape(piece_len, local_heads, HD)
        )
        scores = jnp.einsum("ihd,jhd->hij", query_heads, key_heads) * scale_factor
        scores = scores + bias_now.astype(jnp.float32)
        scores = jnp.where(is_real[None, None, :], scores, -1e30)
        old_peak = jnp.full((local_heads, row_count), -1e30, jnp.float32)
        new_peak = jnp.maximum(old_peak, jnp.max(scores, axis=-1))
        exp_scores = jnp.exp(scores - new_peak[..., None])
        new_total = jnp.sum(exp_scores, axis=-1)
        new_accum = jnp.einsum("hij,jhd->hid", exp_scores, value_heads)
        finished = (new_peak, new_total, new_accum)
        final_peak, final_total, final_accum = finished
        attended = jnp.transpose(final_accum / final_total[..., None], (1, 0, 2)).reshape(
            row_count, local_width
        )
        gated = (attended * jax.nn.sigmoid(gate_vals.astype(jnp.float32))).astype(jnp.bfloat16)
        partial_out = jnp.dot(gated, w_out[layer_index], preferred_element_type=jnp.float32)
        feature_share = lax.psum_scatter(
            partial_out.astype(jnp.bfloat16), "head", scatter_dimension=1, tiled=True
        ).astype(jnp.float32)
        share_width = feature_share.shape[1]
        own_features = lax.dynamic_slice_in_dim(
            state, lax.axis_index("head") * share_width, share_width, 1
        )
        state = lax.all_gather(
            (own_features + query_real[:, None] * feature_share).astype(jnp.bfloat16),
            "head",
            axis=1,
            tiled=True,
        ).astype(jnp.float32)
    return state.astype(jnp.bfloat16)


def solution(mesh):
    placed = (
        P("pb", "head", None),
        P("pb", None),
        P(),
        P(),
        P(),
        P(),
        P(None, None, "head"),
        P(None, None, "head"),
        P(None, None, "head"),
        P(None, None, "head"),
        P(None, "head", None),
    )
    return jax.shard_map(
        on_device, mesh=mesh, in_specs=placed, out_specs=P("pb", None), check_vma=False
    )
```

profile of v0, /device:TPU:0, one launch (start us, length us, event | category | flops | bytes accessed | tf_op | source)
XLA Modules:
  0.0 150.9 jit_solution(16466473360683681310)
XLA Ops:
  6.5 22.2 %while.10 = (s32[]{:T(128)}, bf16[4,32,2048]{2,1,0:T(8,128)(2,1)S(1)}, bf16[4,2048,128]{2,1,0:T(8,128)(2,1)}, bf16[2,128,512]{2,1,0:T(8,128)(2,1)}, bf16[2,256,1...) while((s32[]{:T(128)}, bf16[4,32,2048]{2,1,0:T(8,128)(2,1)S(1)}, ...), condition=%wide.region_9.10_spmd, body=%wide.region_2.9_spmd.sunk | while | flops 836573184 | bytes 30671024 | solution.py:47
  6.5 1.1 constant_dynamic-slice_fusion.2
  8.2 0.7 fusion.123
  9.1 0.8 fusion.124
  10.1 0.7 fusion.125
  10.8 0.8 fusion.126
  11.8 0.2 fusion.127
  12.1 1.1 constant_dynamic-slice_fusion.2
  13.7 0.7 fusion.123
  14.6 0.8 fusion.124
  15.6 0.7 fusion.125
  16.4 0.8 fusion.126
  17.4 0.2 fusion.127
  17.7 1.1 constant_dynamic-slice_fusion.2
  19.3 0.7 fusion.123
  20.2 0.8 fusion.124
  21.2 0.7 fusion.125
  22.0 0.8 fusion.126
  23.0 0.2 fusion.127
  23.2 1.1 constant_dynamic-slice_fusion.2
  24.9 0.7 fusion.123
  25.8 0.8 fusion.124
  26.8 0.7 fusion.125
  27.5 0.8 fusion.126
  28.5 0.2 fusion.127
  29.1 0.9 squeeze.53
  29.9 5.2 %all-to-all-start = ((bf16[16,64,128]{2,1,0:T(8,128)(2,1)}), bf16[16,64,128]{2,1,0:T(8,128)(2,1)S(1)}, u32[]{:S(2)}, u32[]{:S(2)}) async-start(bf16[16,64,128]{2,1,0:T(8,128)(2,1)} %squeeze.53), calls=%async_computation | async-start | bytes 524288 | tf_op jit(solution)/shard_map/all_to_all | solution.py:51
  36.1 14.7 %all_gather.12 = bf16[512,384]{1,0:T(8,128)(2,1)S(1)} all-gather(bf16[64,384]{1,0:T(8,128)(2,1)S(1)} %pad_maximum_fusion), channel_id=1, replica_groups=mesh['head'=4,'pb'=8] {'pb'}, dimensions={0}, use_global_device_ids=true | all-gather | bytes 442368 | tf_op jit(solution)/shard_map/all_gather | solution.py:79
  51.7 0.4 fusion.95
  52.0 0.2 fusion.55
  52.3 0.3 fusion.40
  52.7 1.5 convolution_convert_fusion.2
  54.2 0.8 copy.61
  55.2 0.9 squeeze.59
  56.1 4.2 %all-to-all-start.1 = ((bf16[16,64,128]{2,1,0:T(8,128)(2,1)}), bf16[16,64,128]{2,1,0:T(8,128)(2,1)S(1)}, u32[]{:S(2)}, u32[]{:S(2)}) async-start(bf16[16,64,128]{2,1,0:T(8,128)(2,1)} %squeeze.59), calls=%async_computation.1 | async-start | bytes 524288 | tf_op jit(solution)/shard_map/all_to_all | solution.py:51
  60.4 20.6 %reduce-scatter.7.cloned.1.call-done = bf16[192,64]{1,0:T(8,128)(2,1)} async-done(((bf16[768,64]{1,0:T(8,128)(2,1)}), bf16[192,64]{1,0:T(8,128)(2,1)}) %reduce-scatter.7.cloned.1.call-update) | async-done | bytes 24592
  81.0 0.9 copy.62
  82.0 8.5 %all-gather = bf16[4,192,64]{1,2,0:T(8,128)(2,1)S(1)} all-gather(bf16[1,192,64]{1,2,0:T(8,128)(2,1)S(1)} %fusion.84), channel_id=1, replica_groups=mesh['head'=4,'pb'=8] {'head'}, dimensions={0}, use_global_device_ids=true | all-gather | bytes 122880 | tf_op jit(solution)/shard_map/all_gather | solution.py:109
  91.8 14.5 %all_gather.14 = bf16[512,384]{1,0:T(8,128)(2,1)S(1)} all-gather(bf16[64,384]{1,0:T(8,128)(2,1)S(1)} %pad_maximum_fusion.1), channel_id=1, replica_groups=mesh['head'=4,'pb'=8] {'pb'}, dimensions={0}, use_global_device_ids=true | all-gather | bytes 442368 | tf_op jit(solution)/shard_map/all_gather | solution.py:79
  107.0 0.4 fusion.96
  107.4 0.2 fusion.56
  107.7 0.3 fusion.39
  108.1 0.4 convolution_convert_fusion.1
  108.5 0.8 copy.63
  109.3 24.4 %reduce-scatter.9.cloned.1.call-done = bf16[192,64]{1,0:T(8,128)(2,1)} async-done(((bf16[768,64]{1,0:T(8,128)(2,1)}), bf16[192,64]{1,0:T(8,128)(2,1)}) %reduce-scatter.9.cloned.1.call-update) | async-done | bytes 24592
  133.8 0.9 copy.64
  134.7 8.5 %all-gather.1 = bf16[4,192,64]{1,2,0:T(8,128)(2,1)S(1)} all-gather(bf16[1,192,64]{1,2,0:T(8,128)(2,1)S(1)} %fusion.85), channel_id=1, replica_groups=mesh['head'=4,'pb'=8] {'head'}, dimensions={0}, use_global_device_ids=true | all-gather | bytes 122880 | tf_op jit(solution)/shard_map/all_gather | solution.py:109
  143.3 0.8 reshape.142
  (129 shorter events, 8.3 us)
Async XLA Ops:
  6.5 1.6 %copy-start = (bf16[2,128,512]{2,1,0:T(8,128)(2,1)S(1)}, bf16[2,128,512]{2,1,0:T(8,128)(2,1)}, u32[]{:S(2)}) copy-start(bf16[2,128,512]{2,1,0:T(8,128)(2,1)} %get-tuple-element.144) | copy-start | bytes 786436 | tf_op jit(solution)/shard_map/while
  8.2 0.9 copy-start.9
  10.8 1.0 copy-start.2
  12.1 1.6 %copy-start = (bf16[2,128,512]{2,1,0:T(8,128)(2,1)S(1)}, bf16[2,128,512]{2,1,0:T(8,128)(2,1)}, u32[]{:S(2)}) copy-start(bf16[2,128,512]{2,1,0:T(8,128)(2,1)} %get-tuple-element.144) | copy-start | bytes 786436 | tf_op jit(solution)/shard_map/while
  13.7 0.9 copy-start.9
  16.4 1.0 copy-start.2
  17.6 1.6 %copy-start = (bf16[2,128,512]{2,1,0:T(8,128)(2,1)S(1)}, bf16[2,128,512]{2,1,0:T(8,128)(2,1)}, u32[]{:S(2)}) copy-start(bf16[2,128,512]{2,1,0:T(8,128)(2,1)} %get-tuple-element.144) | copy-start | bytes 786436 | tf_op jit(solution)/shard_map/while
  19.3 0.9 copy-start.9
  21.9 1.0 copy-start.2
  23.2 1.6 %copy-start = (bf16[2,128,512]{2,1,0:T(8,128)(2,1)S(1)}, bf16[2,128,512]{2,1,0:T(8,128)(2,1)}, u32[]{:S(2)}) copy-start(bf16[2,128,512]{2,1,0:T(8,128)(2,1)} %get-tuple-element.144) | copy-start | bytes 786436 | tf_op jit(solution)/shard_map/while
  24.8 0.9 copy-start.9
  27.5 1.0 copy-start.2
  28.7 6.4 %copy-start.1 = (bf16[64,768]{1,0:T(8,128)(2,1)S(1)}, bf16[64,768]{1,0:T(8,128)(2,1)}, u32[]{:S(2)}) copy-start(bf16[64,768]{1,0:T(8,128)(2,1)} %param.14) | copy-start | bytes 294916
  28.8 6.7 %copy-start.4 = (bf16[2,768,192]{1,2,0:T(8,128)(2,1)S(1)}, bf16[2,768,192]{1,2,0:T(8,128)(2,1)}, u32[]{:S(2)}) copy-start(bf16[2,768,192]{1,2,0:T(8,128)(2,1)} %param.21) | copy-start | bytes 1769476
  28.8 7.0 %copy-start.5 = (bf16[2,768,192]{1,2,0:T(8,128)(2,1)S(1)}, bf16[2,768,192]{1,2,0:T(8,128)(2,1)}, u32[]{:S(2)}) copy-start(bf16[2,768,192]{1,2,0:T(8,128)(2,1)} %param.20) | copy-start | bytes 1769476
  29.0 22.1 %copy-start.6 = (bf16[2,768,192]{1,2,0:T(8,128)(2,1)S(1)}, bf16[2,768,192]{1,2,0:T(8,128)(2,1)}, u32[]{:S(2)}) copy-start(bf16[2,768,192]{1,2,0:T(8,128)(2,1)} %param.19) | copy-start | bytes 1769476
  29.9 21.7 %all-to-all-start = ((bf16[16,64,128]{2,1,0:T(8,128)(2,1)}), bf16[16,64,128]{2,1,0:T(8,128)(2,1)S(1)}, u32[]{:S(2)}, u32[]{:S(2)}) async-start(bf16[16,64,128]{2,1,0:T(8,128)(2,1)} %squeeze.53), calls=%async_computation | async-start | bytes 524288 | tf_op jit(solution)/shard_map/all_to_all | solution.py:51
  35.1 45.9 %reduce-scatter.7.cloned.1.call-start = ((), (), s32[]{:S(2)}) async-start(), calls=%async_computation.4 | async-start | bytes 245760
  35.5 16.2 %copy-start.3 = (s32[512]{0:T(512)S(1)}, s32[512]{0:T(512)}, u32[]{:S(2)}) copy-start(s32[512]{0:T(512)} %param.15) | copy-start | bytes 6148
  56.1 51.0 %all-to-all-start.1 = ((bf16[16,64,128]{2,1,0:T(8,128)(2,1)}), bf16[16,64,128]{2,1,0:T(8,128)(2,1)S(1)}, u32[]{:S(2)}, u32[]{:S(2)}) async-start(bf16[16,64,128]{2,1,0:T(8,128)(2,1)} %squeeze.59), calls=%async_computation.1 | async-start | bytes 524288 | tf_op jit(solution)/shard_map/all_to_all | solution.py:51
  60.3 73.5 %reduce-scatter.9.cloned.1.call-start = ((), (), s32[]{:S(2)}) async-start(), calls=%async_computation.5 | async-start | bytes 245760
  106.4 1.7 %copy-start.7 = (bf16[2,192,768]{2,1,0:T(8,128)(2,1)S(1)}, bf16[2,192,768]{2,1,0:T(8,128)(2,1)}, u32[]{:S(2)}) copy-start(bf16[2,192,768]{2,1,0:T(8,128)(2,1)} %param.23) | copy-start | bytes 1769476
  106.4 1.7 %copy-start.8 = (bf16[2,768,192]{1,2,0:T(8,128)(2,1)S(1)}, bf16[2,768,192]{1,2,0:T(8,128)(2,1)}, u32[]{:S(2)}) copy-start(bf16[2,768,192]{1,2,0:T(8,128)(2,1)} %param.22) | copy-start | bytes 1769476
Sparse Core Ops, SparseCore 0:
  55.1 25.8 reduce-scatter.6
  109.5 24.2 reduce-scatter.8
where the time goes:
time: 152 us; the launch traced here: 151 us
  blocking collectives  46.2 us (30%)
  waiting for transfers between devices  45.1 us (30%)
  matrix products  18.1 us (12%)
  local copies, waits for them, and re-layouts  14 us (9%)
  between operations  13.9 us (9%)
  starting transfers between devices  9.39 us (6%)
  other arithmetic  3.75 us (2%)
    unnamed x4, waiting for transfers between devices  45.1 us
    all_gather x2, blocking collectives, on_device(): every_key = lax.all_gather(packed, 'pb', axis=0, tiled=True)  29.2 us
    all_gather x2, blocking collectives, on_device(): lax.all_gather((own_features + query_real[:, None] * feature_share).astyp...  17 us
    all_to_all x2, starting transfers between devices, on_device(): lax.all_to_all(bias_local[layer_index], 'head', split_axis=0, concat_axis...  9.39 us
    dot_general x8, matrix products, transition(): jnp.dot(hidden, w_back, preferred_element_type=jnp.float32)  6.65 us
    dot_general x8, matrix products, transition(): mixed = jnp.dot(normed, w_updown, preferred_element_type=jnp.float32)  5.9 us
    dynamic_slice x8, local copies, waits for them, and re-layouts, on_device(): projected = lax.map(project, blocked)  5.33 us
    unnamed x19, local copies, waits for them, and re-layouts  4.22 us
  transfers between devices with their start and end apart: 4, of which 2 were waited for; matrix products, arithmetic and copies ran while one was open for 4% of the time, Pallas kernels for 0%

commit v1 on v0

v1 whole, which is shorter than its diff:
```python
import functools

import jax
import jax.numpy as jnp
from jax import lax
from jax.experimental import pallas as pl
from jax.experimental.pallas import tpu as pltpu
from jax.sharding import PartitionSpec as P

TRANS = 2
LAYERS = 2
HD = 48
CORES = 2
STEP_ROWS = 16
LANES = 128
F32 = jnp.float32
BF16 = jnp.bfloat16


def normalize(values):
    inverse = 1.0 / values.shape[-1]
    center = values - jnp.sum(values, axis=-1, keepdims=True) * inverse
    spread = jnp.sum(center * center, axis=-1, keepdims=True) * inverse
    return center * lax.rsqrt(spread + 1e-05)


def matmul(left, right):
    return jnp.dot(left, right, preferred_element_type=F32)


def matmul_t(left, right):
    return lax.dot_general(left, right, (((1,), (1,)), ((), ())), preferred_element_type=F32)


def step_kernel(
    head_count,
    pb_count,
    pair_hbm,
    tokens_ref,
    mask_ref,
    gu_ref,
    down_ref,
    bias_w_ref,
    q_hbm,
    k_hbm,
    v_hbm,
    gate_hbm,
    out_hbm,
    result_ref,
    pair_v,
    gu_v,
    wq_v,
    wk_v,
    wv_v,
    wg_v,
    wo_v,
    bias_out,
    bias_in,
    kv_all,
    q_v,
    gate_v,
    sums_out,
    sums_in,
    rows_all,
    pair_sem,
    weight_sem,
    bias_send,
    bias_recv,
    kv_send,
    kv_recv,
    fwd_send,
    fwd_recv,
    sums_send,
    sums_recv,
    rows_send,
    rows_recv,
):
    rows, cols, channels = pair_hbm.shape
    width = q_hbm.shape[2]
    features = tokens_ref.shape[1]
    local_heads = width // HD
    heads_all = local_heads * head_count
    own_rows = rows // head_count
    chips = pb_count // CORES
    col_blocks = cols // LANES
    steps = (rows // STEP_ROWS) * col_blocks
    hidden = down_ref.shape[1]

    head = lax.axis_index("head")
    pb = lax.axis_index("pb")
    core = lax.rem(pb, CORES)
    chip = pb // CORES
    partner = chip * CORES + (1 - core)

    def head_peer(k):
        return lax.rem(head + k, head_count)

    def chip_peer(d):
        return lax.rem(chip + d, chips) * CORES + core

    def chip_source(d):
        return lax.rem(chip + chips - d, chips) * CORES + core

    weight_copies = []
    for index, (source, target) in enumerate(
        ((k_hbm, wk_v), (v_hbm, wv_v), (q_hbm, wq_v), (gate_hbm, wg_v), (out_hbm, wo_v))
    ):
        copy = pltpu.make_async_copy(source, target, weight_sem.at[index])
        copy.start()
        weight_copies.append(copy)

    def pair_copy(n):
        where = (
            pl.ds((n // col_blocks) * STEP_ROWS, STEP_ROWS),
            pl.ds(pl.multiple_of((n % col_blocks) * LANES, LANES), LANES),
        )
        return pltpu.make_async_copy(
            pair_hbm.at[where[0], where[1], :], pair_v.at[where[0], where[1], :], pair_sem.at[n]
        )

    for n in range(steps):
        pair_copy(n).start()

    barrier = pltpu.get_barrier_semaphore()
    for k in range(1, head_count):
        pl.semaphore_signal(
            barrier, inc=1, device_id=(head_peer(k), pb), device_id_type=pl.DeviceIdType.MESH
        )
    for d in range(1, chips):
        pl.semaphore_signal(
            barrier, inc=1, device_id=(head, chip_peer(d)), device_id_type=pl.DeviceIdType.MESH
        )
    pl.semaphore_signal(
        barrier, inc=1, device_id=(head, partner), device_id_type=pl.DeviceIdType.MESH
    )
    pl.semaphore_wait(barrier, head_count + chips - 1)

    def remote(source, target, send, recv, where):
        return pltpu.make_async_remote_copy(
            src_ref=source,
            dst_ref=target,
            send_sem=send,
            recv_sem=recv,
            device_id=where,
            device_id_type=pl.DeviceIdType.MESH,
        )

    def kv_copy(layer, d):
        block = kv_all.at[layer, pb]
        return remote(
            block, block, kv_send.at[layer, d], kv_recv.at[layer, d], (head, chip_peer(d))
        )

    def kv_forward(layer, d):
        block = kv_all.at[layer, chip_source(d)]
        return remote(block, block, fwd_send.at[layer, d], fwd_recv.at[layer, d], (head, partner))

    def project(layer, normed):
        keys = matmul(normed, wk_v[layer]).astype(BF16)
        values = matmul(normed, wv_v[layer]).astype(BF16)
        kv_all[layer, pb] = jnp.concatenate([keys, values], axis=1)
        for d in range(1, chips):
            kv_copy(layer, d).start()
        kv_forward(layer, 0).start()
        q_v[...] = matmul(normed, wq_v[layer]).astype(BF16)
        gate_v[...] = matmul(normed, wg_v[layer]).astype(BF16)

    def forward_kv(layer):
        for d in range(1, chips):
            kv_copy(layer, d).wait_recv()
            kv_forward(layer, d).start()

    def finish_kv(layer):
        for d in range(chips):
            kv_forward(layer, d).wait_recv()

    for copy in weight_copies[:4]:
        copy.wait()
    project(0, normalize(tokens_ref[...].astype(F32)).astype(BF16))

    for section in range(TRANS):
        gu_v[section, :, :hidden] = (gu_ref[section, :, :hidden].astype(F32) * 0.5).astype(BF16)
        gu_v[section, :, hidden:] = gu_ref[section, :, hidden:]
    bias_w = jnp.transpose(bias_w_ref[...].astype(F32)).astype(BF16)

    def bias_copy(n, k):
        where = (
            pl.ds((n // col_blocks) * STEP_ROWS, STEP_ROWS),
            pl.ds(pl.multiple_of((n % col_blocks) * LANES, LANES), LANES),
        )
        return remote(
            bias_out.at[head_peer(k), :, :, where[0], where[1]],
            bias_in.at[head, :, :, where[0], where[1]],
            bias_send.at[n, k],
            bias_recv.at[n, k],
            (head_peer(k), pb),
        )

    half = STEP_ROWS // 2

    def pair_step(n, carry):
        pair_copy(n).wait()
        first_row = (n // col_blocks) * STEP_ROWS
        first_col = pl.multiple_of((n % col_blocks) * LANES, LANES)

        @pl.when(n == steps - 1)
        def _():
            forward_kv(0)

        planes = []
        for part in range(2):
            current = pair_v[
                pl.ds(first_row + part * half, half), pl.ds(first_col, LANES), :
            ].reshape(half * LANES, channels)
            for section in range(TRANS):
                wide = current.astype(F32)
                normed = normalize(wide).astype(BF16)
                mixed = matmul(normed, gu_v[section])
                gate = mixed[:, :hidden]
                units = ((gate + gate * jnp.tanh(gate)) * mixed[:, hidden:]).astype(BF16)
                current = (wide + matmul(units, down_ref[section])).astype(BF16)
            normed = normalize(current.astype(F32)).astype(BF16)
            projected = matmul_t(bias_w, normed)
            planes += [projected[:, i * LANES : (i + 1) * LANES] for i in range(half)]
        by_head = jnp.transpose(jnp.stack(planes, axis=0), (1, 0, 2)).astype(BF16)
        for layer in range(LAYERS):
            for target in range(head_count):
                start = layer * heads_all + target * local_heads
                bias_out[target, layer, :, pl.ds(first_row, STEP_ROWS), pl.ds(first_col, LANES)] = (
                    by_head[start : start + local_heads]
                )
        bias_in[head, :, :, pl.ds(first_row, STEP_ROWS), pl.ds(first_col, LANES)] = bias_out[
            head, :, :, pl.ds(first_row, STEP_ROWS), pl.ds(first_col, LANES)
        ]
        for k in range(1, head_count):
            bias_copy(n, k).start()
        return carry

    lax.fori_loop(0, steps, pair_step, 0)

    mask_row = mask_ref[...]
    real_count = jnp.sum(mask_row.astype(F32), axis=1, keepdims=True)
    is_real = mask_row == 1
    own_first = pb * rows + head * own_rows
    row_index = (lax.broadcasted_iota(jnp.int32, (own_rows, 1), 0) + own_first).astype(F32)
    row_real = (row_index < real_count).astype(F32)
    state = tokens_ref[pl.ds(head * own_rows, own_rows), :].astype(F32)
    lane = lax.broadcasted_iota(jnp.int32, (rows, 2 * width), 1)
    scale = 1.0 / HD**0.5

    def bias_wait(n, carry):
        for k in range(1, head_count):
            bias_copy(n, k).wait_recv()
        return carry

    def sums_copy(layer, k):
        return remote(
            sums_out.at[layer, head_peer(k)],
            sums_in.at[layer, k],
            sums_send.at[layer, k],
            sums_recv.at[layer, k],
            (head_peer(k), pb),
        )

    def rows_copy(layer, k):
        block = rows_all.at[layer, head]
        return remote(
            block, block, rows_send.at[layer, k], rows_recv.at[layer, k], (head_peer(k), pb)
        )

    for layer in range(LAYERS):
        if layer:
            forward_kv(layer)
        finish_kv(layer)
        if not layer:
            lax.fori_loop(0, steps, bias_wait, 0)
            weight_copies[4].wait()
        keys_values = kv_all[layer].reshape(pb_count * rows, 2 * width)
        queries = jnp.concatenate([q_v[...], jnp.zeros((rows, width), BF16)], axis=1)
        spread_q = jnp.concatenate(
            [
                jnp.where((lane >= h * HD) & (lane < (h + 1) * HD), queries, jnp.zeros_like(queries))
                for h in range(local_heads)
            ],
            axis=0,
        )
        bias = jnp.concatenate(
            [
                bias_in[source, layer].reshape(local_heads * rows, cols)
                for source in range(head_count)
            ],
            axis=1,
        )
        scores = matmul_t(spread_q, keys_values) * scale + bias.astype(F32)
        scores = jnp.where(is_real, scores, -1e30)
        peak = jnp.max(scores, axis=1, keepdims=True)
        weights = jnp.exp(scores - peak)
        total = jnp.sum(weights, axis=1, keepdims=True)
        mixed = matmul(weights.astype(BF16), keys_values) / total
        attended = jnp.zeros((rows, 2 * width), F32)
        for h in range(local_heads):
            keep = (lane >= width + h * HD) & (lane < width + (h + 1) * HD)
            attended = attended + jnp.where(keep, mixed[h * rows : (h + 1) * rows], 0.0)
        gated = (attended[:, width:] * jax.nn.sigmoid(gate_v[...].astype(F32))).astype(BF16)
        partial = matmul(gated, wo_v[layer])
        sums_out[layer] = partial.astype(BF16).reshape(head_count, own_rows, features)
        for k in range(1, head_count):
            sums_copy(layer, k).start()
        update = sums_out[layer, head].astype(F32)
        for k in range(1, head_count):
            sums_copy(layer, k).wait_recv()
            update = update + sums_in[layer, k].astype(F32)
        state = state + row_real * update
        last = layer == LAYERS - 1
        rows_all[layer, head] = (state if last else normalize(state)).astype(BF16)
        for k in range(1, head_count):
            rows_copy(layer, k).start()
        for k in range(1, head_count):
            rows_copy(layer, k).wait_recv()
        gathered = rows_all[layer].reshape(rows, features)
        if last:
            result_ref[...] = gathered
        else:
            project(layer + 1, gathered)

    def bias_sent(n, carry):
        for k in range(1, head_count):
            bias_copy(n, k).wait_send()
        return carry

    lax.fori_loop(0, steps, bias_sent, 0)
    for layer in range(LAYERS):
        for d in range(1, chips):
            kv_copy(layer, d).wait_send()
        for d in range(chips):
            kv_forward(layer, d).wait_send()
        for k in range(1, head_count):
            sums_copy(layer, k).wait_send()
            rows_copy(layer, k).wait_send()


def on_device(
    head_count, pb_count, pair, tokens, token_mask, w_gu, w_down, w_bias, w_q, w_k, w_v, w_gate, w_out
):
    rows, cols, channels = pair.shape
    width = w_q.shape[2]
    features = tokens.shape[1]
    local_heads = width // HD
    own_rows = rows // head_count
    chips = pb_count // CORES
    steps = (rows // STEP_ROWS) * (cols // LANES)
    vmem = pl.BlockSpec(memory_space=pltpu.VMEM)
    anywhere = pl.BlockSpec(memory_space=pl.ANY)
    dma = pltpu.SemaphoreType.DMA
    bias_shape = (head_count, LAYERS, local_heads, rows, cols)
    return pl.pallas_call(
        functools.partial(step_kernel, head_count, pb_count),
        out_shape=jax.ShapeDtypeStruct((rows, features), BF16),
        in_specs=[anywhere] + [vmem] * 5 + [anywhere] * 5,
        out_specs=vmem,
        scratch_shapes=[
            pltpu.VMEM(pair.shape, BF16),
            pltpu.VMEM(w_gu.shape, BF16),
            pltpu.VMEM(w_q.shape, BF16),
            pltpu.VMEM(w_k.shape, BF16),
            pltpu.VMEM(w_v.shape, BF16),
            pltpu.VMEM(w_gate.shape, BF16),
            pltpu.VMEM(w_out.shape, BF16),
            pltpu.VMEM(bias_shape, BF16),
            pltpu.VMEM(bias_shape, BF16),
            pltpu.VMEM((LAYERS, pb_count, rows, 2 * width), BF16),
            pltpu.VMEM((rows, width), BF16),
            pltpu.VMEM((rows, width), BF16),
            pltpu.VMEM((LAYERS, head_count, own_rows, features), BF16),
            pltpu.VMEM((LAYERS, head_count, own_rows, features), BF16),
            pltpu.VMEM((LAYERS, head_count, own_rows, features), BF16),
            dma((steps,)),
            dma((5,)),
            dma((steps, head_count)),
            dma((steps, head_count)),
            dma((LAYERS, chips)),
            dma((LAYERS, chips)),
            dma((LAYERS, chips)),
            dma((LAYERS, chips)),
            dma((LAYERS, head_count)),
            dma((LAYERS, head_count)),
            dma((LAYERS, head_count)),
            dma((LAYERS, head_count)),
        ],
        compiler_params=pltpu.CompilerParams(
            collective_id=0, has_side_effects=True, vmem_limit_bytes=60 * 1024 * 1024
        ),
        name="diffusion_step",
    )(
        pair,
        tokens,
        token_mask.reshape(1, -1),
        w_gu,
        w_down,
        w_bias,
        w_q,
        w_k,
        w_v,
        w_gate,
        w_out,
    )


def solution(mesh):
    placed = (
        P("pb", "head", None),
        P("pb", None),
        P(),
        P(),
        P(),
        P(),
        P(None, None, "head"),
        P(None, None, "head"),
        P(None, None, "head"),
        P(None, None, "head"),
        P(None, "head", None),
    )
    return jax.shard_map(
        functools.partial(on_device, mesh.shape["head"], mesh.shape["pb"]),
        mesh=mesh,
        in_specs=placed,
        out_specs=P("pb", None),
        check_vma=False,
    )
```

time: 152 us -> 60.4 us (0.40)
  Pallas kernels: 0 us -> 50.3 us
  blocking collectives: 46.2 us -> 0 us
  waiting for transfers between devices: 45.1 us -> 0 us
  matrix products: 18.1 us -> 0 us
  between operations: 13.9 us -> 0.01 us
  starting transfers between devices: 9.39 us -> 0 us
  local copies, waits for them, and re-layouts: 14 us -> 9.84 us
  other arithmetic: 3.75 us -> 0 us
    pallas_call x0 -> x1, Pallas kernels: none -> 50.3 us  [on_device(): pl.pallas_call(functools.partial(step_kernel, head_count, pb_count), out_...]
    all_gather x4 -> x0, blocking collectives: 46.2 us -> none  [the longest x2 29.2 us: on_device(): every_key = lax.all_gather(packed, 'pb', axis=0, tiled=True)]
    unnamed x4 -> x0, waiting for transfers between devices: 45.1 us -> none
    dot_general x32 -> x0, matrix products: 18.1 us -> none  [the longest x8 6.65 us: transition(): jnp.dot(hidden, w_back, preferred_element_type=jnp.float32)]
    all_to_all x2 -> x0, starting transfers between devices: 9.39 us -> none  [on_device(): lax.all_to_all(bias_local[layer_index], 'head', split_axis=0, concat_axis...]
    unnamed x19 -> x10, local copies, waits for them, and re-layouts: 4.22 us -> 9.84 us
    dynamic_slice x8 -> x0, local copies, waits for them, and re-layouts: 5.33 us -> none  [on_device(): projected = lax.map(project, blocked)]
    reduce_sum x22 -> x0, other arithmetic: 3.05 us -> none  [the longest x14 2.01 us: normalize(): spread = jnp.mean(center * center, axis=-1, keepdims=True)]
  transfers between devices with their start and end apart: 4 -> 0, of which waited for: 2 -> 0; matrix products, arithmetic and copies ran while one was open for 4% -> 0% of each run, Pallas kernels for 0% -> 0%
where the time goes in v1:
time: 60.4 us; the launch traced here: 60.2 us
  Pallas kernels  50.3 us (83%)
  local copies, waits for them, and re-layouts  9.84 us (16%)
    pallas_call x1, Pallas kernels, on_device(): pl.pallas_call(functools.partial(step_kernel, head_count, pb_count), out_...  50.3 us
    unnamed x10, local copies, waits for them, and re-layouts  9.84 us

profile of v1, /device:TPU:0, one launch (start us, length us, event | category | flops | bytes accessed | tf_op | source)
XLA Modules:
  0.0 60.2 jit_solution(9741559801676516564)
XLA Ops:
  0.0 0.0 copy-start.1
  0.0 0.0 copy-start
  0.0 1.5 %copy.12.bias_w_ref = bf16[128,32]{1,0:T(8,128)(2,1)} copy(bf16[128,32]{0,1:T(8,128)(2,1)} %param.16) | data formatting | bytes 16384 | tf_op args[5]
  1.5 2.2 %copy.13.q_hbm = bf16[2,768,192]{2,1,0:T(8,128)(2,1)} copy(bf16[2,768,192]{1,2,0:T(8,128)(2,1)} %param.17) | data formatting | bytes 1179648 | tf_op args[6]
  3.7 2.2 %copy.14.k_hbm = bf16[2,768,192]{2,1,0:T(8,128)(2,1)} copy(bf16[2,768,192]{1,2,0:T(8,128)(2,1)} %param.18) | data formatting | bytes 1179648 | tf_op args[7]
  6.0 0.0 copy-done
  6.0 1.2 %copy.15.v_hbm = bf16[2,768,192]{2,1,0:T(8,128)(2,1)} copy(bf16[2,768,192]{1,2,0:T(8,128)(2,1)S(1)} %copy-done) | data formatting | bytes 1179648 | tf_op args[8]
  7.1 0.0 copy-done.1
  7.1 1.2 %copy.16.gate_hbm = bf16[2,768,192]{2,1,0:T(8,128)(2,1)} copy(bf16[2,768,192]{1,2,0:T(8,128)(2,1)S(1)} %copy-done.1) | data formatting | bytes 1179648 | tf_op args[9]
  8.3 50.3 %diffusion_step.1 = bf16[64,768]{1,0:T(8,128)(2,1)} custom-call(bf16[64,128,128]{2,1,0:T(8,128)(2,1)} %pair_hbm.1, bf16[64,768]{1,0:T(8,128)(2,1)} %tokens_ref.1, s32[1,512]{1,0:T(1,128)} %bitcast.1, bf16[2,128,512]{2,1,0:T(8,128)(2,1)} %gu_ref.1, bf16[2,256,128]{2,1,0:T(8,128)(2,1)} %down_ref.1, bf16[128,32]{1,0:T(8,128)(2,1)} %copy.12.bias_w_ref, ...), custom_call_target="tpu_custom_call" | custom-call | tf_op jit(solution)/shard_map/diffusion_step/pallas_call | solution.py:356
  58.6 1.5 %copy.18 = bf16[64,768]{1,0:T(8,128)(2,1)} copy(bf16[64,768]{1,0:T(8,128)(2,1)} %diffusion_step.1) | data formatting | bytes 196608
Async XLA Ops:
  0.0 7.1 %copy-start.1 = (bf16[2,768,192]{1,2,0:T(8,128)(2,1)S(1)}, bf16[2,768,192]{1,2,0:T(8,128)(2,1)}, u32[]{:S(2)}) copy-start(bf16[2,768,192]{1,2,0:T(8,128)(2,1)} %param.20) | copy-start | bytes 1769476
  0.0 6.0 %copy-start = (bf16[2,768,192]{1,2,0:T(8,128)(2,1)S(1)}, bf16[2,768,192]{1,2,0:T(8,128)(2,1)}, u32[]{:S(2)}) copy-start(bf16[2,768,192]{1,2,0:T(8,128)(2,1)} %param.19) | copy-start | bytes 1769476

commit v2 on v1

--- a/solution.py
+++ b/solution.py
@@ -49,19 +49,13 @@
     result_ref,
     pair_v,
     gu_v,
-    wq_v,
-    wk_v,
-    wv_v,
-    wg_v,
-    wo_v,
+    wide_w,
+    out_w,
     bias_out,
     bias_in,
     kv_all,
-    q_v,
-    gate_v,
-    sums_out,
-    sums_in,
-    rows_all,
+    query_gate,
+    gated_all,
     pair_sem,
     weight_sem,
     bias_send,
@@ -70,17 +64,19 @@
     kv_recv,
     fwd_send,
     fwd_recv,
-    sums_send,
-    sums_recv,
-    rows_send,
-    rows_recv,
+    gated_send,
+    gated_recv,
+    out_send,
+    out_recv,
+    out_fwd_send,
+    out_fwd_recv,
 ):
     rows, cols, channels = pair_hbm.shape
-    width = q_hbm.shape[2]
+    width = q_hbm.shape[1]
     features = tokens_ref.shape[1]
     local_heads = width // HD
     heads_all = local_heads * head_count
-    own_rows = rows // head_count
+    half_width = width // CORES
     chips = pb_count // CORES
     col_blocks = cols // LANES
     steps = (rows // STEP_ROWS) * col_blocks
@@ -101,13 +97,24 @@
     def chip_source(d):
         return lax.rem(chip + chips - d, chips) * CORES + core
 
-    weight_copies = []
-    for index, (source, target) in enumerate(
-        ((k_hbm, wk_v), (v_hbm, wv_v), (q_hbm, wq_v), (gate_hbm, wg_v), (out_hbm, wo_v))
-    ):
-        copy = pltpu.make_async_copy(source, target, weight_sem.at[index])
-        copy.start()
-        weight_copies.append(copy)
+    def weight_copies(layer):
+        copies = [
+            pltpu.make_async_copy(
+                source.at[layer],
+                wide_w.at[layer, index * width : (index + 1) * width],
+                weight_sem.at[layer, index],
+            )
+            for index, source in enumerate((k_hbm, v_hbm, q_hbm, gate_hbm))
+        ]
+        for part in range(CORES):
+            copies.append(
+                pltpu.make_async_copy(
+                    out_hbm.at[layer, part * half_width : (part + 1) * half_width],
+                    out_w.at[layer, head, part],
+                    weight_sem.at[layer, 4 + part],
+                )
+            )
+        return copies
 
     def pair_copy(n):
         where = (
@@ -118,8 +125,12 @@
             pair_hbm.at[where[0], where[1], :], pair_v.at[where[0], where[1], :], pair_sem.at[n]
         )
 
+    for copy in weight_copies(0)[:4]:
+        copy.start()
     for n in range(steps):
         pair_copy(n).start()
+    for copy in weight_copies(0)[4:] + weight_copies(1):
+        copy.start()
 
     barrier = pltpu.get_barrier_semaphore()
     for k in range(1, head_count):
@@ -133,7 +144,6 @@
     pl.semaphore_signal(
         barrier, inc=1, device_id=(head, partner), device_id_type=pl.DeviceIdType.MESH
     )
-    pl.semaphore_wait(barrier, head_count + chips - 1)
 
     def remote(source, target, send, recv, where):
         return pltpu.make_async_remote_copy(
@@ -155,15 +165,45 @@
         block = kv_all.at[layer, chip_source(d)]
         return remote(block, block, fwd_send.at[layer, d], fwd_recv.at[layer, d], (head, partner))
 
+    def out_copy(layer, k):
+        return remote(
+            out_hbm.at[layer, pl.ds(pl.multiple_of(core * half_width, half_width), half_width)],
+            out_w.at[layer, head, core],
+            out_send.at[layer, k],
+            out_recv.at[layer, k],
+            (head_peer(k), pb),
+        )
+
+    def out_forward(layer, k):
+        block = out_w.at[layer, lax.rem(head + head_count - k, head_count), core]
+        return remote(
+            block, block, out_fwd_send.at[layer, k], out_fwd_recv.at[layer, k], (head, partner)
+        )
+
+    def forward_out():
+        for layer in range(LAYERS):
+            for k in range(1, head_count):
+                out_copy(layer, k).wait_recv()
+                out_forward(layer, k).start()
+
+    def gated_copy(layer, k):
+        block = gated_all.at[layer, head]
+        return remote(
+            block, block, gated_send.at[layer, k], gated_recv.at[layer, k], (head_peer(k), pb)
+        )
+
     def project(layer, normed):
-        keys = matmul(normed, wk_v[layer]).astype(BF16)
-        values = matmul(normed, wv_v[layer]).astype(BF16)
-        kv_all[layer, pb] = jnp.concatenate([keys, values], axis=1)
+        kv_all[layer, pb] = matmul_t(normed, wide_w[layer, : 2 * width]).astype(BF16)
+        if not layer:
+            pl.semaphore_wait(barrier, head_count + chips - 1)
         for d in range(1, chips):
             kv_copy(layer, d).start()
         kv_forward(layer, 0).start()
-        q_v[...] = matmul(normed, wq_v[layer]).astype(BF16)
-        gate_v[...] = matmul(normed, wg_v[layer]).astype(BF16)
+        if not layer:
+            for which in range(LAYERS):
+                for k in range(1, head_count):
+                    out_copy(which, k).start()
+        query_gate[...] = matmul_t(normed, wide_w[layer, 2 * width :]).astype(BF16)
 
     def forward_kv(layer):
         for d in range(1, chips):
@@ -174,14 +214,14 @@
         for d in range(chips):
             kv_forward(layer, d).wait_recv()
 
-    for copy in weight_copies[:4]:
+    for copy in weight_copies(0)[:4]:
         copy.wait()
     project(0, normalize(tokens_ref[...].astype(F32)).astype(BF16))
 
     for section in range(TRANS):
         gu_v[section, :, :hidden] = (gu_ref[section, :, :hidden].astype(F32) * 0.5).astype(BF16)
         gu_v[section, :, hidden:] = gu_ref[section, :, hidden:]
-    bias_w = jnp.transpose(bias_w_ref[...].astype(F32)).astype(BF16)
+    bias_w = bias_w_ref[...]
 
     def bias_copy(n, k):
         where = (
@@ -206,6 +246,7 @@
         @pl.when(n == steps - 1)
         def _():
             forward_kv(0)
+            forward_out()
 
         planes = []
         for part in range(2):
@@ -241,10 +282,9 @@
     mask_row = mask_ref[...]
     real_count = jnp.sum(mask_row.astype(F32), axis=1, keepdims=True)
     is_real = mask_row == 1
-    own_first = pb * rows + head * own_rows
-    row_index = (lax.broadcasted_iota(jnp.int32, (own_rows, 1), 0) + own_first).astype(F32)
+    row_index = (lax.broadcasted_iota(jnp.int32, (rows, 1), 0) + pb * rows).astype(F32)
     row_real = (row_index < real_count).astype(F32)
-    state = tokens_ref[pl.ds(head * own_rows, own_rows), :].astype(F32)
+    state = tokens_ref[...].astype(F32)
     lane = lax.broadcasted_iota(jnp.int32, (rows, 2 * width), 1)
     scale = 1.0 / HD**0.5
 
@@ -252,21 +292,6 @@
         for k in range(1, head_count):
             bias_copy(n, k).wait_recv()
         return carry
-
-    def sums_copy(layer, k):
-        return remote(
-            sums_out.at[layer, head_peer(k)],
-            sums_in.at[layer, k],
-            sums_send.at[layer, k],
-            sums_recv.at[layer, k],
-            (head_peer(k), pb),
-        )
-
-    def rows_copy(layer, k):
-        block = rows_all.at[layer, head]
-        return remote(
-            block, block, rows_send.at[layer, k], rows_recv.at[layer, k], (head_peer(k), pb)
-        )
 
     for layer in range(LAYERS):
         if layer:
@@ -274,9 +299,8 @@
         finish_kv(layer)
         if not layer:
             lax.fori_loop(0, steps, bias_wait, 0)
-            weight_copies[4].wait()
         keys_values = kv_all[layer].reshape(pb_count * rows, 2 * width)
-        queries = jnp.concatenate([q_v[...], jnp.zeros((rows, width), BF16)], axis=1)
+        queries = query_gate[...]
         spread_q = jnp.concatenate(
             [
                 jnp.where((lane >= h * HD) & (lane < (h + 1) * HD), queries, jnp.zeros_like(queries))
@@ -301,27 +325,25 @@
         for h in range(local_heads):
             keep = (lane >= width + h * HD) & (lane < width + (h + 1) * HD)
             attended = attended + jnp.where(keep, mixed[h * rows : (h + 1) * rows], 0.0)
-        gated = (attended[:, width:] * jax.nn.sigmoid(gate_v[...].astype(F32))).astype(BF16)
-        partial = matmul(gated, wo_v[layer])
-        sums_out[layer] = partial.astype(BF16).reshape(head_count, own_rows, features)
-        for k in range(1, head_count):
-            sums_copy(layer, k).start()
-        update = sums_out[layer, head].astype(F32)
-        for k in range(1, head_count):
-            sums_copy(layer, k).wait_recv()
-            update = update + sums_in[layer, k].astype(F32)
+        gated = (attended * jax.nn.sigmoid(queries.astype(F32))).astype(BF16)
+        gated_all[layer, head] = gated[:, width:]
+        for k in range(1, head_count):
+            gated_copy(layer, k).start()
+        for k in range(1, head_count):
+            out_forward(layer, k).wait_recv()
+        for copy in weight_copies(layer)[4:]:
+            copy.wait()
+        for k in range(1, head_count):
+            gated_copy(layer, k).wait_recv()
+        gathered = jnp.concatenate([gated_all[layer, h] for h in range(head_count)], axis=1)
+        update = matmul(gathered, out_w[layer].reshape(head_count * width, features))
         state = state + row_real * update
-        last = layer == LAYERS - 1
-        rows_all[layer, head] = (state if last else normalize(state)).astype(BF16)
-        for k in range(1, head_count):
-            rows_copy(layer, k).start()
-        for k in range(1, head_count):
-            rows_copy(layer, k).wait_recv()
-        gathered = rows_all[layer].reshape(rows, features)
-        if last:
-            result_ref[...] = gathered
+        if layer == LAYERS - 1:
+            result_ref[...] = state.astype(BF16)
         else:
-            project(layer + 1, gathered)
+            for copy in weight_copies(layer + 1)[:4]:
+                copy.wait()
+            project(layer + 1, normalize(state).astype(BF16))
 
     def bias_sent(n, carry):
         for k in range(1, head_count):
@@ -335,8 +357,9 @@
         for d in range(chips):
             kv_forward(layer, d).wait_send()
         for k in range(1, head_count):
-            sums_copy(layer, k).wait_send()
-            rows_copy(layer, k).wait_send()
+            gated_copy(layer, k).wait_send()
+            out_copy(layer, k).wait_send()
+            out_forward(layer, k).wait_send()
 
 
 def on_device(
@@ -346,7 +369,6 @@
     width = w_q.shape[2]
     features = tokens.shape[1]
     local_heads = width // HD
-    own_rows = rows // head_count
     chips = pb_count // CORES
     steps = (rows // STEP_ROWS) * (cols // LANES)
     vmem = pl.BlockSpec(memory_space=pltpu.VMEM)
@@ -361,27 +383,23 @@
         scratch_shapes=[
             pltpu.VMEM(pair.shape, BF16),
             pltpu.VMEM(w_gu.shape, BF16),
-            pltpu.VMEM(w_q.shape, BF16),
-            pltpu.VMEM(w_k.shape, BF16),
-            pltpu.VMEM(w_v.shape, BF16),
-            pltpu.VMEM(w_gate.shape, BF16),
-            pltpu.VMEM(w_out.shape, BF16),
+            pltpu.VMEM((LAYERS, 4 * width, features), BF16),
+            pltpu.VMEM((LAYERS, head_count, CORES, width // CORES, features), BF16),
             pltpu.VMEM(bias_shape, BF16),
             pltpu.VMEM(bias_shape, BF16),
             pltpu.VMEM((LAYERS, pb_count, rows, 2 * width), BF16),
-            pltpu.VMEM((rows, width), BF16),
-            pltpu.VMEM((rows, width), BF16),
-            pltpu.VMEM((LAYERS, head_count, own_rows, features), BF16),
-            pltpu.VMEM((LAYERS, head_count, own_rows, features), BF16),
-            pltpu.VMEM((LAYERS, head_count, own_rows, features), BF16),
+            pltpu.VMEM((rows, 2 * width), BF16),
+            pltpu.VMEM((LAYERS, head_count, rows, width), BF16),
             dma((steps,)),
-            dma((5,)),
+            dma((LAYERS, 4 + CORES)),
             dma((steps, head_count)),
             dma((steps, head_count)),
             dma((LAYERS, chips)),
             dma((LAYERS, chips)),
             dma((LAYERS, chips)),
             dma((LAYERS, chips)),
+            dma((LAYERS, head_count)),
+            dma((LAYERS, head_count)),
             dma((LAYERS, head_count)),
             dma((LAYERS, head_count)),
             dma((LAYERS, head_count)),
@@ -397,11 +415,11 @@
         token_mask.reshape(1, -1),
         w_gu,
         w_down,
-        w_bias,
-        w_q,
-        w_k,
-        w_v,
-        w_gate,
+        w_bias.T,
+        jnp.swapaxes(w_q, 1, 2),
+        jnp.swapaxes(w_k, 1, 2),
+        jnp.swapaxes(w_v, 1, 2),
+        jnp.swapaxes(w_gate, 1, 2),
         w_out,
     )
 

time: 60.4 us -> 47.9 us (0.79)
  local copies, waits for them, and re-layouts: 9.84 us -> 1.54 us
  Pallas kernels: 50.3 us -> 46.2 us
    unnamed x10 -> x1, local copies, waits for them, and re-layouts: 9.84 us -> 1.54 us
    pallas_call x1, Pallas kernels: 50.3 us -> 46.2 us  [on_device(): pl.pallas_call(functools.partial(step_kernel, head_count, pb_count), out_...]
where the time goes in v2:
time: 47.9 us; the launch traced here: 47.7 us
  Pallas kernels  46.2 us (96%)
  local copies, waits for them, and re-layouts  1.54 us (3%)
    pallas_call x1, Pallas kernels, on_device(): pl.pallas_call(functools.partial(step_kernel, head_count, pb_count), out_...  46.2 us
    unnamed x1, local copies, waits for them, and re-layouts  1.54 us

profile of v2, /device:TPU:0, one launch (start us, length us, event | category | flops | bytes accessed | tf_op | source)
XLA Modules:
  0.0 47.7 jit_solution(3492475204141028916)
XLA Ops:
  0.0 46.2 %diffusion_step.1 = bf16[64,768]{1,0:T(8,128)(2,1)} custom-call(bf16[64,128,128]{2,1,0:T(8,128)(2,1)} %pair_hbm.1, bf16[64,768]{1,0:T(8,128)(2,1)} %tokens_ref.1, s32[1,512]{1,0:T(1,128)} %bitcast.11, bf16[2,128,512]{2,1,0:T(8,128)(2,1)} %gu_ref.1, bf16[2,256,128]{2,1,0:T(8,128)(2,1)} %down_ref.1, bf16[32,128]{1,0:T(8,128)(2,1)} %bitcast.10, ...), custom_call_target="tpu_custom_call" | custom-call | tf_op jit(solution)/shard_map/diffusion_step/pallas_call | solution.py:378
  46.2 1.5 %copy.13 = bf16[64,768]{1,0:T(8,128)(2,1)} copy(bf16[64,768]{1,0:T(8,128)(2,1)} %diffusion_step.1) | data formatting | bytes 196608

commit v3 on v2

--- a/solution.py
+++ b/solution.py
@@ -21,6 +21,14 @@
     inverse = 1.0 / values.shape[-1]
     center = values - jnp.sum(values, axis=-1, keepdims=True) * inverse
     spread = jnp.sum(center * center, axis=-1, keepdims=True) * inverse
+    return center * lax.rsqrt(spread + 1e-05)
+
+
+def normalize_wide(values):
+    inverse = 1.0 / values.shape[-1]
+    center = values - jnp.sum(values, axis=-1, keepdims=True) * inverse
+    ones = jnp.full((values.shape[-1], values.shape[-1]), inverse, BF16)
+    spread = matmul((center * center).astype(BF16), ones)
     return center * lax.rsqrt(spread + 1e-05)
 
 
@@ -97,8 +105,8 @@
     def chip_source(d):
         return lax.rem(chip + chips - d, chips) * CORES + core
 
-    def weight_copies(layer):
-        copies = [
+    def projection_copies(layer):
+        return [
             pltpu.make_async_copy(
                 source.at[layer],
                 wide_w.at[layer, index * width : (index + 1) * width],
@@ -106,15 +114,16 @@
             )
             for index, source in enumerate((k_hbm, v_hbm, q_hbm, gate_hbm))
         ]
-        for part in range(CORES):
-            copies.append(
-                pltpu.make_async_copy(
-                    out_hbm.at[layer, part * half_width : (part + 1) * half_width],
-                    out_w.at[layer, head, part],
-                    weight_sem.at[layer, 4 + part],
-                )
+
+    def own_out_copies(layer):
+        return [
+            pltpu.make_async_copy(
+                out_hbm.at[layer, part * half_width : (part + 1) * half_width],
+                out_w.at[layer, head, part],
+                weight_sem.at[layer, 4 + part],
             )
-        return copies
+            for part in range(CORES)
+        ]
 
     def pair_copy(n):
         where = (
@@ -125,12 +134,14 @@
             pair_hbm.at[where[0], where[1], :], pair_v.at[where[0], where[1], :], pair_sem.at[n]
         )
 
-    for copy in weight_copies(0)[:4]:
+    pair_copy(0).start()
+    for copy in projection_copies(0):
         copy.start()
-    for n in range(steps):
+    for n in range(1, steps):
         pair_copy(n).start()
-    for copy in weight_copies(0)[4:] + weight_copies(1):
-        copy.start()
+    for layer in range(LAYERS):
+        for copy in own_out_copies(layer) + (projection_copies(layer) if layer else []):
+            copy.start()
 
     barrier = pltpu.get_barrier_semaphore()
     for k in range(1, head_count):
@@ -180,11 +191,10 @@
             block, block, out_fwd_send.at[layer, k], out_fwd_recv.at[layer, k], (head, partner)
         )
 
-    def forward_out():
-        for layer in range(LAYERS):
-            for k in range(1, head_count):
-                out_copy(layer, k).wait_recv()
-                out_forward(layer, k).start()
+    def forward_out(layer):
+        for k in range(1, head_count):
+            out_copy(layer, k).wait_recv()
+            out_forward(layer, k).start()
 
     def gated_copy(layer, k):
         block = gated_all.at[layer, head]
@@ -200,9 +210,8 @@
             kv_copy(layer, d).start()
         kv_forward(layer, 0).start()
         if not layer:
-            for which in range(LAYERS):
-                for k in range(1, head_count):
-                    out_copy(which, k).start()
+            for k in range(1, head_count):
+                out_copy(0, k).start()
         query_gate[...] = matmul_t(normed, wide_w[layer, 2 * width :]).astype(BF16)
 
     def forward_kv(layer):
@@ -214,25 +223,21 @@
         for d in range(chips):
             kv_forward(layer, d).wait_recv()
 
-    for copy in weight_copies(0)[:4]:
-        copy.wait()
-    project(0, normalize(tokens_ref[...].astype(F32)).astype(BF16))
-
     for section in range(TRANS):
         gu_v[section, :, :hidden] = (gu_ref[section, :, :hidden].astype(F32) * 0.5).astype(BF16)
         gu_v[section, :, hidden:] = gu_ref[section, :, hidden:]
     bias_w = bias_w_ref[...]
 
-    def bias_copy(n, k):
+    def bias_copy(n, layer, k):
         where = (
             pl.ds((n // col_blocks) * STEP_ROWS, STEP_ROWS),
             pl.ds(pl.multiple_of((n % col_blocks) * LANES, LANES), LANES),
         )
         return remote(
-            bias_out.at[head_peer(k), :, :, where[0], where[1]],
-            bias_in.at[head, :, :, where[0], where[1]],
-            bias_send.at[n, k],
-            bias_recv.at[n, k],
+            bias_out.at[head_peer(k), layer, :, where[0], where[1]],
+            bias_in.at[head, layer, :, where[0], where[1]],
+            bias_send.at[n, layer, k],
+            bias_recv.at[n, layer, k],
             (head_peer(k), pb),
         )
 
@@ -242,11 +247,6 @@
         pair_copy(n).wait()
         first_row = (n // col_blocks) * STEP_ROWS
         first_col = pl.multiple_of((n % col_blocks) * LANES, LANES)
-
-        @pl.when(n == steps - 1)
-        def _():
-            forward_kv(0)
-            forward_out()
 
         planes = []
         for part in range(2):
@@ -255,12 +255,12 @@
             ].reshape(half * LANES, channels)
             for section in range(TRANS):
                 wide = current.astype(F32)
-                normed = normalize(wide).astype(BF16)
+                normed = normalize_wide(wide).astype(BF16)
                 mixed = matmul(normed, gu_v[section])
                 gate = mixed[:, :hidden]
                 units = ((gate + gate * jnp.tanh(gate)) * mixed[:, hidden:]).astype(BF16)
                 current = (wide + matmul(units, down_ref[section])).astype(BF16)
-            normed = normalize(current.astype(F32)).astype(BF16)
+            normed = normalize_wide(current.astype(F32)).astype(BF16)
             projected = matmul_t(bias_w, normed)
             planes += [projected[:, i * LANES : (i + 1) * LANES] for i in range(half)]
         by_head = jnp.transpose(jnp.stack(planes, axis=0), (1, 0, 2)).astype(BF16)
@@ -273,8 +273,22 @@
         bias_in[head, :, :, pl.ds(first_row, STEP_ROWS), pl.ds(first_col, LANES)] = bias_out[
             head, :, :, pl.ds(first_row, STEP_ROWS), pl.ds(first_col, LANES)
         ]
-        for k in range(1, head_count):
-            bias_copy(n, k).start()
+
+        @pl.when(n == 0)
+        def _():
+            for copy in projection_copies(0):
+                copy.wait()
+            project(0, normalize(tokens_ref[...].astype(F32)).astype(BF16))
+
+        for layer in range(LAYERS):
+            for k in range(1, head_count):
+                bias_copy(n, layer, k).start()
+
+        @pl.when(n == steps - 2)
+        def _():
+            forward_kv(0)
+            forward_out(0)
+
         return carry
 
     lax.fori_loop(0, steps, pair_step, 0)
@@ -288,17 +302,15 @@
     lane = lax.broadcasted_iota(jnp.int32, (rows, 2 * width), 1)
     scale = 1.0 / HD**0.5
 
-    def bias_wait(n, carry):
-        for k in range(1, head_count):
-            bias_copy(n, k).wait_recv()
+    def bias_wait(layer, n, carry):
+        for k in range(1, head_count):
+            bias_copy(n, layer, k).wait_recv()
         return carry
 
     for layer in range(LAYERS):
         if layer:
             forward_kv(layer)
         finish_kv(layer)
-        if not layer:
-            lax.fori_loop(0, steps, bias_wait, 0)
         keys_values = kv_all[layer].reshape(pb_count * rows, 2 * width)
         queries = query_gate[...]
         spread_q = jnp.concatenate(
@@ -308,6 +320,8 @@
             ],
             axis=0,
         )
+        scores = matmul_t(spread_q, keys_values) * scale
+        lax.fori_loop(0, steps, functools.partial(bias_wait, layer), 0)
         bias = jnp.concatenate(
             [
                 bias_in[source, layer].reshape(local_heads * rows, cols)
@@ -315,7 +329,7 @@
             ],
             axis=1,
         )
-        scores = matmul_t(spread_q, keys_values) * scale + bias.astype(F32)
+        scores = scores + bias.astype(F32)
         scores = jnp.where(is_real, scores, -1e30)
         peak = jnp.max(scores, axis=1, keepdims=True)
         weights = jnp.exp(scores - peak)
@@ -329,25 +343,31 @@
         gated_all[layer, head] = gated[:, width:]
         for k in range(1, head_count):
             gated_copy(layer, k).start()
+        if layer:
+            forward_out(layer)
         for k in range(1, head_count):
             out_forward(layer, k).wait_recv()
-        for copy in weight_copies(layer)[4:]:
+        for copy in own_out_copies(layer):
             copy.wait()
         for k in range(1, head_count):
             gated_copy(layer, k).wait_recv()
+        if layer + 1 < LAYERS:
+            for k in range(1, head_count):
+                out_copy(layer + 1, k).start()
         gathered = jnp.concatenate([gated_all[layer, h] for h in range(head_count)], axis=1)
         update = matmul(gathered, out_w[layer].reshape(head_count * width, features))
         state = state + row_real * update
         if layer == LAYERS - 1:
             result_ref[...] = state.astype(BF16)
         else:
-            for copy in weight_copies(layer + 1)[:4]:
+            for copy in projection_copies(layer + 1):
                 copy.wait()
             project(layer + 1, normalize(state).astype(BF16))
 
     def bias_sent(n, carry):
-        for k in range(1, head_count):
-            bias_copy(n, k).wait_send()
+        for layer in range(LAYERS):
+            for k in range(1, head_count):
+                bias_copy(n, layer, k).wait_send()
         return carry
 
     lax.fori_loop(0, steps, bias_sent, 0)
@@ -392,8 +412,8 @@
             pltpu.VMEM((LAYERS, head_count, rows, width), BF16),
             dma((steps,)),
             dma((LAYERS, 4 + CORES)),
-            dma((steps, head_count)),
-            dma((steps, head_count)),
+            dma((steps, LAYERS, head_count)),
+            dma((steps, LAYERS, head_count)),
             dma((LAYERS, chips)),
             dma((LAYERS, chips)),
             dma((LAYERS, chips)),

time: 47.9 us -> 45.7 us (0.954)
  Pallas kernels: 46.2 us -> 44 us
    pallas_call x1, Pallas kernels: 46.2 us -> 44 us  [on_device(): pl.pallas_call(functools.partial(step_kernel, head_count, pb_count), out_...]
where the time goes in v3:
time: 45.7 us; the launch traced here: 45.6 us
  Pallas kernels  44 us (96%)
  local copies, waits for them, and re-layouts  1.54 us (3%)
    pallas_call x1, Pallas kernels, on_device(): pl.pallas_call(functools.partial(step_kernel, head_count, pb_count), out_...  44 us
    unnamed x1, local copies, waits for them, and re-layouts  1.54 us

profile of v3, /device:TPU:0, one launch (start us, length us, event | category | flops | bytes accessed | tf_op | source)
XLA Modules:
  0.0 45.6 jit_solution(461004477517149037)
XLA Ops:
  0.0 44.0 %diffusion_step.1 = bf16[64,768]{1,0:T(8,128)(2,1)} custom-call(bf16[64,128,128]{2,1,0:T(8,128)(2,1)} %pair_hbm.1, bf16[64,768]{1,0:T(8,128)(2,1)} %tokens_ref.1, s32[1,512]{1,0:T(1,128)} %bitcast.11, bf16[2,128,512]{2,1,0:T(8,128)(2,1)} %gu_ref.1, bf16[2,256,128]{2,1,0:T(8,128)(2,1)} %down_ref.1, bf16[32,128]{1,0:T(8,128)(2,1)} %bitcast.10, ...), custom_call_target="tpu_custom_call" | custom-call | tf_op jit(solution)/shard_map/diffusion_step/pallas_call | solution.py:398
  44.0 1.5 %copy.13 = bf16[64,768]{1,0:T(8,128)(2,1)} copy(bf16[64,768]{1,0:T(8,128)(2,1)} %diffusion_step.1) | data formatting | bytes 196608

commit v4 on v3

--- a/solution.py
+++ b/solution.py
@@ -44,17 +44,21 @@
     head_count,
     pb_count,
     pair_hbm,
-    tokens_ref,
+    tokens_hbm,
     mask_ref,
-    gu_ref,
-    down_ref,
-    bias_w_ref,
+    gu_hbm,
+    down_hbm,
+    bias_w_hbm,
     q_hbm,
     k_hbm,
     v_hbm,
     gate_hbm,
     out_hbm,
     result_ref,
+    tokens_ref,
+    gu_ref,
+    down_ref,
+    bias_w_ref,
     pair_v,
     gu_v,
     wide_w,
@@ -66,6 +70,7 @@
     gated_all,
     pair_sem,
     weight_sem,
+    small_sem,
     bias_send,
     bias_recv,
     kv_send,
@@ -105,6 +110,19 @@
     def chip_source(d):
         return lax.rem(chip + chips - d, chips) * CORES + core
 
+    barrier = pltpu.get_barrier_semaphore()
+    for k in range(1, head_count):
+        pl.semaphore_signal(
+            barrier, inc=1, device_id=(head_peer(k), pb), device_id_type=pl.DeviceIdType.MESH
+        )
+    for d in range(1, chips):
+        pl.semaphore_signal(
+            barrier, inc=1, device_id=(head, chip_peer(d)), device_id_type=pl.DeviceIdType.MESH
+        )
+    pl.semaphore_signal(
+        barrier, inc=1, device_id=(head, partner), device_id_type=pl.DeviceIdType.MESH
+    )
+
     def projection_copies(layer):
         return [
             pltpu.make_async_copy(
@@ -134,27 +152,26 @@
             pair_hbm.at[where[0], where[1], :], pair_v.at[where[0], where[1], :], pair_sem.at[n]
         )
 
+    small_copies = [
+        pltpu.make_async_copy(source, target, small_sem.at[index])
+        for index, (source, target) in enumerate(
+            (
+                (gu_hbm, gu_ref),
+                (down_hbm, down_ref),
+                (bias_w_hbm, bias_w_ref),
+                (tokens_hbm, tokens_ref),
+            )
+        )
+    ]
+    small_copies[0].start()
     pair_copy(0).start()
-    for copy in projection_copies(0):
+    for copy in small_copies[1:] + projection_copies(0):
         copy.start()
     for n in range(1, steps):
         pair_copy(n).start()
     for layer in range(LAYERS):
         for copy in own_out_copies(layer) + (projection_copies(layer) if layer else []):
             copy.start()
-
-    barrier = pltpu.get_barrier_semaphore()
-    for k in range(1, head_count):
-        pl.semaphore_signal(
-            barrier, inc=1, device_id=(head_peer(k), pb), device_id_type=pl.DeviceIdType.MESH
-        )
-    for d in range(1, chips):
-        pl.semaphore_signal(
-            barrier, inc=1, device_id=(head, chip_peer(d)), device_id_type=pl.DeviceIdType.MESH
-        )
-    pl.semaphore_signal(
-        barrier, inc=1, device_id=(head, partner), device_id_type=pl.DeviceIdType.MESH
-    )
 
     def remote(source, target, send, recv, where):
         return pltpu.make_async_remote_copy(
@@ -222,6 +239,9 @@
     def finish_kv(layer):
         for d in range(chips):
             kv_forward(layer, d).wait_recv()
+
+    for copy in small_copies:
+        copy.wait()
 
     for section in range(TRANS):
         gu_v[section, :, :hidden] = (gu_ref[section, :, :hidden].astype(F32) * 0.5).astype(BF16)
@@ -398,9 +418,13 @@
     return pl.pallas_call(
         functools.partial(step_kernel, head_count, pb_count),
         out_shape=jax.ShapeDtypeStruct((rows, features), BF16),
-        in_specs=[anywhere] + [vmem] * 5 + [anywhere] * 5,
+        in_specs=[anywhere, anywhere, vmem] + [anywhere] * 8,
         out_specs=vmem,
         scratch_shapes=[
+            pltpu.VMEM(tokens.shape, BF16),
+            pltpu.VMEM(w_gu.shape, BF16),
+            pltpu.VMEM(w_down.shape, BF16),
+            pltpu.VMEM(w_bias.shape[::-1], BF16),
             pltpu.VMEM(pair.shape, BF16),
             pltpu.VMEM(w_gu.shape, BF16),
             pltpu.VMEM((LAYERS, 4 * width, features), BF16),
@@ -412,6 +436,7 @@
             pltpu.VMEM((LAYERS, head_count, rows, width), BF16),
             dma((steps,)),
             dma((LAYERS, 4 + CORES)),
+            dma((4,)),
             dma((steps, LAYERS, head_count)),
             dma((steps, LAYERS, head_count)),
             dma((LAYERS, chips)),

time: 45.7 us -> 46.5 us (1.018)
  Pallas kernels: 44 us -> 44.8 us
    pallas_call x1, Pallas kernels: 44 us -> 44.8 us  [on_device(): pl.pallas_call(functools.partial(step_kernel, head_count, pb_count), out_...]
where the time goes in v4:
time: 46.5 us; the launch traced here: 46.4 us
  Pallas kernels  44.8 us (96%)
  local copies, waits for them, and re-layouts  1.54 us (3%)
    pallas_call x1, Pallas kernels, on_device(): pl.pallas_call(functools.partial(step_kernel, head_count, pb_count), out_...  44.8 us
    unnamed x1, local copies, waits for them, and re-layouts  1.54 us

profile of v4, /device:TPU:0, one launch (start us, length us, event | category | flops | bytes accessed | tf_op | source)
XLA Modules:
  0.0 46.4 jit_solution(8408638450580115196)
XLA Ops:
  0.0 44.8 %diffusion_step.1 = bf16[64,768]{1,0:T(8,128)(2,1)} custom-call(bf16[64,128,128]{2,1,0:T(8,128)(2,1)} %pair_hbm.1, bf16[64,768]{1,0:T(8,128)(2,1)} %tokens_hbm.1, s32[1,512]{1,0:T(1,128)} %bitcast.11, bf16[2,128,512]{2,1,0:T(8,128)(2,1)} %gu_hbm.1, bf16[2,256,128]{2,1,0:T(8,128)(2,1)} %down_hbm.1, bf16[32,128]{1,0:T(8,128)(2,1)} %bitcast.10, ...), custom_call_target="tpu_custom_call" | custom-call | tf_op jit(solution)/shard_map/diffusion_step/pallas_call | solution.py:418
  44.8 1.5 %copy.13 = bf16[64,768]{1,0:T(8,128)(2,1)} copy(bf16[64,768]{1,0:T(8,128)(2,1)} %diffusion_step.1) | data formatting | bytes 196608
